TPU v7x, 256 devices: a whole 4x4x8 slice. The times are simulated.
256 devices in a mesh: child: 2 (over y_hi), row: 32 (over z, y_lo, core), col: 4 (over x).
Axes of the slice: x: 4, y: 4 (y_hi: 2, y_lo: 2; y = y_hi * 2 + y_lo), z: 8, core: 2. Of those that a mesh axis runs over, the one named last changes fastest.
Arguments:
- front: bfloat16 [131072, 2048], P(('row', 'child'), 'col'), as said below
- left_factors: bfloat16 [2, 4, 64, 131072], P('child', 'col', None, 'row'), may hold values from -2.5 to 2.5
- right_factors: bfloat16 [2, 256, 64, 2048], P('child', 'row', None, 'col'), may hold values from -2.5 to 2.5
Outputs:
- panel_t: bfloat16 [2048, 131072], P('col', ('row', 'child'))
Inputs may be any that keep to these rules, and one draw needn't show every extreme that they name: The first 2048 rows of front make the symmetric part of the assembled diagonal block positive definite: its diagonal entries exceed the spectral norm of the rest of that part several times.
All inputs are finite; a program needn't handle non-finite values.
Results may differ from a plain program's by a relative error of at most 0.012.
Values may be sent and summed in bfloat16 or wider, within the bound.
No kernel may reach another device: no remote copies, remote signals or barrier semaphores. Data moves between devices by JAX's collectives and lax.ppermute only.
A program may use at most 128 MiB of HBM per device.

v0:
```python
import jax
import jax.numpy as jnp
from jax import lax
from jax.sharding import PartitionSpec as P

TILE = 512
RANK = 64
PW = 2048


def shortened(array):

    def short(part):
        return part.astype(jnp.bfloat16) if part.dtype == jnp.float32 else part

    return jax.tree.map(short, array)


def spread(value, axis, source):
    kept = jnp.where(lax.axis_index(axis) == source, value, 0).astype(value.dtype)
    return lax.psum(kept, axis)


def product_high(left, right):
    return jnp.dot(left, right, precision=lax.Precision.HIGHEST)


def inverse_transpose(top):
    blocks = PW // TILE
    identity = jnp.eye(TILE, dtype=jnp.float32)

    def tile_of(i, j):
        return top[i * TILE : (i + 1) * TILE, j * TILE : (j + 1) * TILE].astype(jnp.float32)

    def sym_tile(i, j):
        return 0.5 * (tile_of(i, j) + tile_of(j, i).T)

    lower = {}
    diag_inv = {}
    for j in range(blocks):
        accum = sym_tile(j, j)
        for k in range(j):
            accum = accum - product_high(lower[j, k], lower[j, k].T)
        lower[j, j] = jnp.linalg.cholesky(accum)
        diag_inv[j] = lax.linalg.triangular_solve(lower[j, j], identity, left_side=True, lower=True)
        for i in range(j + 1, blocks):
            accum = sym_tile(i, j)
            for k in range(j):
                accum = accum - product_high(lower[i, k], lower[j, k].T)
            lower[i, j] = product_high(accum, diag_inv[j].T)
    pieces = {}
    for i in range(blocks):
        pieces[i, i] = diag_inv[i]
    for i in range(blocks):
        for j in range(i):
            acc = jnp.zeros((TILE, TILE), jnp.float32)
            for k in range(j, i):
                acc = acc + product_high(lower[i, k], pieces[k, j])
            pieces[i, j] = -product_high(pieces[i, i], acc)
    zero_tile = jnp.zeros((TILE, TILE), jnp.bfloat16)
    row_list = [
        jnp.concatenate(
            [pieces[b, a].T.astype(jnp.bfloat16) if a <= b else zero_tile for b in range(blocks)],
            axis=1,
        )
        for a in range(blocks)
    ]
    return jnp.concatenate(row_list, axis=0)


def child_term(left_part, right_part):
    left_tiles = left_part.reshape(RANK, right_part.shape[0], TILE)
    result = jnp.einsum("rtk,trn->tkn", left_tiles, right_part, preferred_element_type=jnp.float32)
    return result.reshape(-1, TILE)


def shards(front, left_factors, right_factors):
    side = lax.axis_index("child")
    left_all = left_factors[0, 0]
    right_all = right_factors[0]
    update = lax.psum_scatter(
        child_term(left_all, right_all).astype(jnp.bfloat16),
        "child",
        scatter_dimension=0,
        tiled=True,
    ).astype(jnp.float32)
    panel_rows = (front.astype(jnp.float32) - update).astype(jnp.bfloat16)
    column = lax.axis_index("col")
    is_root = jnp.logical_and(side == 0, lax.axis_index("row") == 0)
    top = lax.all_gather(panel_rows[:PW], "col", axis=1, tiled=True)

    def select_block(matrix):
        return lax.dynamic_slice_in_dim(matrix, column * TILE, TILE, 0)

    empty_shape = (TILE, PW)
    local_block = lax.cond(
        is_root,
        lambda t: select_block(inverse_transpose(t)),
        lambda t: jnp.zeros(empty_shape, jnp.bfloat16),
        top,
    )
    inverse_block = jax.tree.map(
        lambda part, own: part.astype(own.dtype),
        jax.tree.map(lambda part: spread(part, ("child", "row"), 0), shortened(local_block)),
        local_block,
    )
    part = lax.slice_in_dim(inverse_block, 0, lax.axis_size("col") * TILE, axis=1)
    panel_t = lax.psum_scatter(
        lax.dot_general(
            part, panel_rows, (((0,), (1,)), ((), ())), preferred_element_type=jnp.float32
        ),
        "col",
        scatter_dimension=0,
        tiled=True,
    )
    return panel_t.astype(jnp.bfloat16)


def solution(mesh):
    in_specs = (
        P(("row", "child"), "col"),
        P("child", "col", None, "row"),
        P("child", "row", None, "col"),
    )
    out_specs = P("col", ("row", "child"))
    return jax.shard_map(shards, mesh=mesh, in_specs=in_specs, out_specs=out_specs, check_vma=False)
```

profile of v0, /device:TPU:1, one launch (start us, length us, event | category | flops | bytes accessed | tf_op | source)
XLA Modules:
  0.0 1288.6 jit_solution(6734739488787908376)
XLA Ops:
  6.5 1.3 copy.31
  7.8 0.0 copy-done
  7.8 0.0 copy-start.46
  7.8 3.2 convolution_convert_fusion
  11.1 0.0 reduce-scatter.3.cloned.1.call-update
  11.1 0.0 all-gather.2.cloned.1.call-start
  11.1 64.8 %reduce-scatter.3.cloned.1.call-done = bf16[2048,512]{1,0:T(8,128)(2,1)} async-done(((bf16[4096,512]{1,0:T(8,128)(2,1)}), bf16[2048,512]{1,0:T(8,128)(2,1)}) %reduce-scatter.3.cloned.1.call-update) | async-done | bytes 2097168 | tf_op jit(solution)/shard_map/reduce_scatter | solution.py:81
  76.0 3.5 subtract_convert_fusion
  79.5 0.0 all-gather.2.cloned.1.call-update
  79.5 0.0 all-reduce.4.cloned.1.call-start
  79.5 85.1 %all-gather.2.cloned.1.call-done = bf16[2048,2048]{1,0:T(8,128)(2,1)} async-done(((bf16[2048,512]{1,0:T(8,128)(2,1)}), bf16[2048,2048]{1,0:T(8,128)(2,1)}) %all-gather.2.cloned.1.call-update) | async-done | bytes 8388624 | tf_op jit(solution)/shard_map/all_gather | solution.py:90
  164.7 1.5 conditional.1
  164.7 1.5 broadcast.134
  166.2 1.5 broadcast_select_fusion
  167.7 0.0 all-reduce.4.cloned.1.call-update
  167.7 0.0 reduce-scatter.5.cloned.1.call-start
  167.8 949.7 %all-reduce.4.cloned.1.call-done = bf16[512,2048]{0,1:T(8,128)(2,1)} async-done(((bf16[512,2048]{0,1:T(8,128)(2,1)}), bf16[512,2048]{0,1:T(8,128)(2,1)}) %all-reduce.4.cloned.1.call-update) | async-done | bytes 2097168 | tf_op jit(solution)/shard_map/psum | solution.py:21
  1117.5 0.0 copy-done.35
  1117.5 9.7 fusion.185
  1127.2 0.0 reduce-scatter.5.cloned.1.call-update
  1127.2 0.0 copy-start.1
  1127.2 151.0 %reduce-scatter.5.cloned.1.call-done = f32[512,2048]{1,0:T(8,128)} async-done(((f32[2048,2048]{1,0:T(8,128)}), f32[512,2048]{1,0:T(8,128)}) %reduce-scatter.5.cloned.1.call-update) | async-done | bytes 4194320 | tf_op jit(solution)/shard_map/reduce_scatter | solution.py:108
  1278.2 3.8 convert_element_type.129
  1282.1 0.0 copy-done.1
  (4 shorter events, 0.0 us)
Async XLA Ops:
  6.5 1.3 copy-start
  6.5 69.4 %reduce-scatter.3.cloned.1.call-start = ((), (), s32[]{:S(2)}) async-start(), calls=%async_computation.2 | async-start | bytes 6291456 | tf_op jit(solution)/shard_map/reduce_scatter | solution.py:81
  7.8 68.1 %copy-start.46 = (bf16[2048,512]{1,0:T(8,128)(2,1)S(1)}, bf16[2048,512]{1,0:T(8,128)(2,1)}, u32[]{:S(2)}) copy-start(bf16[2048,512]{1,0:T(8,128)(2,1)} %param.8) | copy-start | bytes 6291460
  11.1 153.6 %all-gather.2.cloned.1.call-start = ((), (), s32[]{:S(2)}) async-start(), calls=%async_computation.3 | async-start | bytes 10485760 | tf_op jit(solution)/shard_map/all_gather | solution.py:90
  79.5 1038.0 %all-reduce.4.cloned.1.call-start = ((), (), s32[]{:S(2)}) async-start(), calls=%async_computation.4 | async-start | bytes 4194304 | tf_op jit(solution)/shard_map/psum | solution.py:21
  166.2 951.3 %copy-start.35 = (bf16[2048,512]{1,0:T(8,128)(2,1)S(1)}, bf16[2048,512]{1,0:T(8,128)(2,1)}, u32[]{:S(2)}) copy-start(bf16[2048,512]{1,0:T(8,128)(2,1)} %subtract_convert_fusion) | copy-start | bytes 6291460
  167.7 1110.5 %reduce-scatter.5.cloned.1.call-start = ((), (), s32[]{:S(2)}) async-start(), calls=%async_computation.5 | async-start | bytes 20971520 | tf_op jit(solution)/shard_map/reduce_scatter | solution.py:108
  1127.2 154.8 %copy-start.1 = (bf16[1,8,64,512]{3,2,1,0:T(8,128)(2,1)S(1)}, bf16[1,8,64,512]{3,2,1,0:T(8,128)(2,1)}, u32[]{:S(2)}) copy-start(bf16[1,8,64,512]{3,2,1,0:T(8,128)(2,1)} %param.10) | copy-start | bytes 1572868
Sparse Core Ops, SparseCore 0:
  11.2 64.6 reduce-scatter.2
  79.6 85.0 all-gather.1
  168.5 948.9 all-reduce.3
  1127.3 150.8 reduce-scatter.4
where the time goes:
time: 1290 us
  waiting for transfers between devices  1250 us (97%)
  between operations  13.2 us (1%)
  matrix products  12.9 us (1%)
    psum x1, waiting for transfers between devices, spread(): return lax.psum(kept, axis)  950 us
    reduce_scatter x1, waiting for transfers between devices, shards(): lax.psum_scatter(lax.dot_general(part, panel_rows, (((0,), (1,)), ((), ()...  151 us
    all_gather x1, waiting for transfers between devices, shards(): top = lax.all_gather(panel_rows[:PW], 'col', axis=1, tiled=True)  85.1 us
    reduce_scatter x1, waiting for transfers between devices, shards(): lax.psum_scatter(child_term(left_all, right_all).astype(jnp.bfloat16), 'c...  64.8 us
  transfers between devices with their start and end apart: 4, of which 4 were waited for; matrix products, arithmetic and copies ran while one was open for 0% of the time, Pallas kernels for 0%

commit v1 on v0

--- a/solution.py
+++ b/solution.py
@@ -6,6 +6,24 @@
 TILE = 512
 RANK = 64
 PW = 2048
+
+
+def ring_gather(array, axis, dim):
+    ways, here, step = (lax.axis_size(axis), lax.axis_index(axis), array.shape[dim])
+    dims = [n * ways if d == dim else n for d, n in enumerate(array.shape)]
+    full = lax.dynamic_update_slice_in_dim(
+        jnp.zeros(dims, array.dtype), array, here * step, axis=dim
+    )
+    going_up = going_down = array
+    for far in range(1, ways // 2 + 1):
+        going_up = lax.ppermute(going_up, axis, [(d, (d + 1) % ways) for d in range(ways)])
+        full = lax.dynamic_update_slice_in_dim(full, going_up, (here - far) % ways * step, axis=dim)
+        if 2 * far < ways:
+            going_down = lax.ppermute(going_down, axis, [(d, (d - 1) % ways) for d in range(ways)])
+            full = lax.dynamic_update_slice_in_dim(
+                full, going_down, (here + far) % ways * step, axis=dim
+            )
+    return full
 
 
 def shortened(array):
@@ -87,7 +105,7 @@
     panel_rows = (front.astype(jnp.float32) - update).astype(jnp.bfloat16)
     column = lax.axis_index("col")
     is_root = jnp.logical_and(side == 0, lax.axis_index("row") == 0)
-    top = lax.all_gather(panel_rows[:PW], "col", axis=1, tiled=True)
+    top = ring_gather(panel_rows[:PW], "col", 1)
 
     def select_block(matrix):
         return lax.dynamic_slice_in_dim(matrix, column * TILE, TILE, 0)

time: 1290 us -> 1340 us (1.039)
  waiting for transfers between devices: 1250 us -> 1290 us
    ppermute x0 -> x3, waiting for transfers between devices: none -> 92 us  [the longest x2 92 us: ring_gather(): lax.ppermute(going_up, axis, [(d, (d + 1) % ways) for d in range(ways)])]
    all_gather x1 -> x0, waiting for transfers between devices: 85.1 us -> none  [shards(): top = lax.all_gather(panel_rows[:PW], 'col', axis=1, tiled=True)]
    psum x1, waiting for transfers between devices: 950 us -> 982 us  [spread(): return lax.psum(kept, axis)]
  transfers between devices with their start and end apart: 4 -> 6, of which waited for: 4 -> 5; matrix products, arithmetic and copies ran while one was open for 0% -> 0% of each run, Pallas kernels for 0% -> 0%
where the time goes in v1:
time: 1340 us; the launch traced here: 1330 us
  waiting for transfers between devices  1290 us (96%)
  matrix products  15.7 us (1%)
    psum x1, waiting for transfers between devices, spread(): return lax.psum(kept, axis)  982 us
    reduce_scatter x1, waiting for transfers between devices, shards(): lax.psum_scatter(lax.dot_general(part, panel_rows, (((0,), (1,)), ((), ()...  151 us
    ppermute x2, waiting for transfers between devices, ring_gather(): lax.ppermute(going_up, axis, [(d, (d + 1) % ways) for d in range(ways)])  92 us
    reduce_scatter x1, waiting for transfers between devices, shards(): lax.psum_scatter(child_term(left_all, right_all).astype(jnp.bfloat16), 'c...  64.8 us
  transfers between devices with their start and end apart: 6, of which 5 were waited for; matrix products, arithmetic and copies ran while one was open for 0% of the time, Pallas kernels for 0%

profile of v1, /device:TPU:1, one launch (start us, length us, event | category | flops | bytes accessed | tf_op | source)
XLA Modules:
  0.0 1331.7 jit_solution(7496000228711934007)
XLA Ops:
  6.5 1.3 copy.88
  7.8 0.0 copy-start.41
  7.8 3.2 convolution_convert_fusion
  11.1 0.0 reduce-scatter.3.cloned.1.call-update
  11.1 0.0 all-reduce.4.cloned.1.call-start
  11.1 64.8 %reduce-scatter.3.cloned.1.call-done = bf16[2048,512]{1,0:T(8,128)(2,1)} async-done(((bf16[4096,512]{1,0:T(8,128)(2,1)}), bf16[2048,512]{1,0:T(8,128)(2,1)}) %reduce-scatter.3.cloned.1.call-update) | async-done | bytes 2097168 | tf_op jit(solution)/shard_map/reduce_scatter | solution.py:99
  76.0 3.5 subtract_convert_fusion
  79.5 1.2 collective-permute-start
  80.7 1.5 collective-permute-start.1
  82.1 45.2 %collective-permute-done = bf16[2048,512]{1,0:T(8,128)(2,1)S(1)} collective-permute-done((bf16[2048,512]{1,0:T(8,128)(2,1)}, bf16[2048,512]{1,0:T(8,128)(2,1)S(1)}, u32[]{:S(2)}, u32[]{:S(2)}) %collective-permute-start) | collective-permute-done | bytes 2097184 | tf_op jit(solution)/shard_map/ppermute | solution.py:19
  127.3 0.1 collective-permute-start.2
  127.5 0.0 collective-permute-done.1
  127.5 46.7 %collective-permute-done.2 = bf16[2048,512]{1,0:T(8,128)(2,1)} collective-permute-done((bf16[2048,512]{1,0:T(8,128)(2,1)S(1)}, bf16[2048,512]{1,0:T(8,128)(2,1)}, u32[]{:S(2)}, u32[]{:S(2)}) %collective-permute-start.2) | collective-permute-done | bytes 2097184 | tf_op jit(solution)/shard_map/ppermute | solution.py:19
  174.2 0.4 conditional.1
  174.2 0.1 broadcast.146
  174.6 1.5 broadcast_select_fusion
  176.1 0.0 all-reduce.4.cloned.1.call-update
  176.1 0.0 reduce-scatter.5.cloned.1.call-start
  176.2 981.7 %all-reduce.4.cloned.1.call-done = bf16[512,2048]{0,1:T(8,128)(2,1)} async-done(((bf16[512,2048]{0,1:T(8,128)(2,1)}), bf16[512,2048]{0,1:T(8,128)(2,1)}) %all-reduce.4.cloned.1.call-update) | async-done | bytes 2097168 | tf_op jit(solution)/shard_map/psum | solution.py:39
  1157.8 12.5 fusion.181
  1170.3 0.0 reduce-scatter.5.cloned.1.call-update
  1170.3 0.0 copy-start.1
  1170.3 151.0 %reduce-scatter.5.cloned.1.call-done = f32[512,2048]{1,0:T(8,128)} async-done(((f32[2048,2048]{1,0:T(8,128)}), f32[512,2048]{1,0:T(8,128)}) %reduce-scatter.5.cloned.1.call-update) | async-done | bytes 4194320 | tf_op jit(solution)/shard_map/reduce_scatter | solution.py:126
  1321.3 3.8 convert_element_type.210
  (5 shorter events, 0.0 us)
Async XLA Ops:
  6.5 1.3 copy-start
  6.5 69.4 %reduce-scatter.3.cloned.1.call-start = ((), (), s32[]{:S(2)}) async-start(), calls=%async_computation.2 | async-start | bytes 6291456 | tf_op jit(solution)/shard_map/reduce_scatter | solution.py:99
  7.8 68.1 %copy-start.41 = (bf16[2048,512]{1,0:T(8,128)(2,1)S(1)}, bf16[2048,512]{1,0:T(8,128)(2,1)}, u32[]{:S(2)}) copy-start(bf16[2048,512]{1,0:T(8,128)(2,1)} %param.8) | copy-start | bytes 6291460
  11.1 1146.7 %all-reduce.4.cloned.1.call-start = ((), (), s32[]{:S(2)}) async-start(), calls=%async_computation.3 | async-start | bytes 4194304 | tf_op jit(solution)/shard_map/psum | solution.py:39
  79.5 47.9 %collective-permute-start = (bf16[2048,512]{1,0:T(8,128)(2,1)}, bf16[2048,512]{1,0:T(8,128)(2,1)S(1)}, u32[]{:S(2)}, u32[]{:S(2)}) collective-permute-start(bf16[2048,512]{1,0:T(8,128)(2,1)} %subtract_convert_fusion), channel_id=1, source_target_pairs={{0,1},{1,2},{2,3},{3,0},{4,5},{5,6},{6,7},{7,4},{8,9},{9,10},{10,1... | collective-permute-start | bytes 6291464 | tf_op jit(solution)/shard_map/ppermute | solution.py:19
  80.7 46.8 %collective-permute-start.1 = (bf16[2048,512]{1,0:T(8,128)(2,1)}, bf16[2048,512]{1,0:T(8,128)(2,1)}, u32[]{:S(2)}, u32[]{:S(2)}) collective-permute-start(bf16[2048,512]{1,0:T(8,128)(2,1)} %subtract_convert_fusion), channel_id=1, source_target_pairs={{0,3},{1,0},{2,1},{3,2},{4,7},{5,4},{6,5},{7,6},{8,11},{9,8},{10,9... | collective-permute-start | bytes 6291464 | tf_op jit(solution)/shard_map/ppermute | solution.py:22
  127.3 46.9 %collective-permute-start.2 = (bf16[2048,512]{1,0:T(8,128)(2,1)S(1)}, bf16[2048,512]{1,0:T(8,128)(2,1)}, u32[]{:S(2)}, u32[]{:S(2)}) collective-permute-start(bf16[2048,512]{1,0:T(8,128)(2,1)S(1)} %collective-permute-done), channel_id=1, source_target_pairs={{0,1},{1,2},{2,3},{3,0},{4,5},{5,6},{6,7},{7,4},{8,9},{9,10},{10,1... | collective-permute-start | bytes 6291464 | tf_op jit(solution)/shard_map/ppermute | solution.py:19
  176.1 1145.2 %reduce-scatter.5.cloned.1.call-start = ((), (), s32[]{:S(2)}) async-start(), calls=%async_computation.4 | async-start | bytes 20971520 | tf_op jit(solution)/shard_map/reduce_scatter | solution.py:126
  1170.3 154.8 %copy-start.1 = (bf16[1,8,64,512]{3,2,1,0:T(8,128)(2,1)S(1)}, bf16[1,8,64,512]{3,2,1,0:T(8,128)(2,1)}, u32[]{:S(2)}) copy-start(bf16[1,8,64,512]{3,2,1,0:T(8,128)(2,1)} %param.10) | copy-start | bytes 1572868
Sparse Core Ops, SparseCore 0:
  11.2 64.6 reduce-scatter.2
  176.2 981.5 all-reduce.3
  1170.5 150.8 reduce-scatter.4
